TPU v7x, 256 devices: a whole 4x4x8 slice. The times are simulated.
256 devices in a mesh: row: 8 (over y, core), col: 32 (over x, z).
Axes of the slice: x: 4, y: 4, z: 8, core: 2. Of those that a mesh axis runs over, the one named last changes fastest.
Arguments:
- kkt: float32 [8192, 8192], P('row', 'col'), may hold values from -4 to 4, as said below
- swaps: int32 [2, 2, 128], replicated, may hold values from 0 to 8191, as said below
- inverses: float32 [2, 256, 256], replicated
- pivots: float32 [2, 256], replicated, may hold values from -0.12 to 0.12
- couplings: float32 [2, 256], replicated, may hold values from -0.12 to 0.12
- pattern: int32 [2, 256], replicated, may hold values from 0 to 1, as said below
Outputs:
- factored: float32 [8192, 8192], P('row', 'col')
Inputs may be any that keep to these rules, and one draw needn't show every extreme that they name: For panel k, swaps[k, 0, :] holds 128 distinct rows among k * 256 to k * 256 + 255, both ends of that range among them, and swaps[k, 1, :] holds 128 distinct rows among (k + 1) * 256 to 8191, both ends of that range among them. pattern[k, i] = 1 makes rows i and i + 1 one 2 x 2 block of D; no two neighbouring entries are both 1 and the last entry is 0. kkt is the stored order of a symmetric matrix.
All inputs are finite; a program needn't handle non-finite values.
Results may differ from a plain program's by a relative error of at most 0.00014.
Values sent between devices are 32-bit elements; how exact they have to be, the bound alone decides.
A program may use at most 64 MiB of HBM per device.

v0:
```python
import jax
import jax.numpy as jnp
from jax import lax
from jax.sharding import Mesh
from jax.sharding import PartitionSpec as P

COL = ("col_0", "col_1")
HI = lax.Precision.HIGHEST


def tdot(a, b):
    return lax.dot_general(
        a, b, (((0,), (0,)), ((), ())), precision=HI, preferred_element_type=jnp.float32
    )


def swapped(rows, lead, partner):
    to_partner = rows[:, None] == lead[None, :]
    to_lead = rows[:, None] == partner[None, :]
    moved = jnp.sum(
        jnp.where(to_partner, partner[None, :], 0) + jnp.where(to_lead, lead[None, :], 0), axis=1
    )
    return jnp.where(jnp.any(to_partner | to_lead, axis=1), moved, rows)


def plan(swaps, tile, row_groups, dtype=jnp.float32):
    width = tile // row_groups
    count = swaps.shape[2]
    partner = swaps[:, 1, :].reshape(-1)
    top = jnp.arange(2 * tile, dtype=jnp.int32)
    rows = jnp.concatenate([top, partner])
    source = swapped(swapped(rows, swaps[1, 0], swaps[1, 1]), swaps[0, 0], swaps[0, 1])
    repeated = jnp.any(swaps[0, 1][:, None] == swaps[1, 1][None, :], axis=1)
    valid = jnp.concatenate([~repeated, jnp.ones((count,), bool)]) & (partner >= 2 * tile)
    sliced = source.reshape(3, row_groups, width).transpose(1, 0, 2)
    return (rows, source, sliced, jnp.where(valid, partner, -1))


def hits(rows, first, tile):
    return (rows[:, None] == first + jnp.arange(tile, dtype=jnp.int32)[None, :]).astype(jnp.float32)


def along_d(lower_t, pivot, coupling, pattern):
    links = coupling * pattern.astype(jnp.float32)
    zero = jnp.zeros((1, lower_t.shape[1]), lower_t.dtype)
    after = jnp.concatenate([lower_t[1:], zero], axis=0)
    before = jnp.concatenate([zero, lower_t[:-1]], axis=0)
    links_before = jnp.concatenate([jnp.zeros((1,), links.dtype), links[:-1]])
    return lower_t * pivot[:, None] + after * links[:, None] + before * links_before[:, None]


def exchange(picked, moves, tile, row_groups, x_size):
    width = tile // row_groups
    row_index = lax.axis_index("row")
    z_index = lax.axis_index("col_1")
    piece = lax.psum_scatter(picked, "row", scatter_dimension=0, tiled=False)
    strip = lax.all_gather(piece, "row")
    mine = lax.psum(jnp.where(z_index == row_index, strip, 0.0), "col_1")
    wide = lax.all_gather(mine, "col_0")
    part = jnp.dot(piece, moves, precision=HI, preferred_element_type=jnp.float32)
    t0, t1, tp = (part[:width], part[width : 2 * width], part[2 * width :])
    corner = jnp.stack(
        [
            t0[:, 2 * tile :],
            t1[:, 2 * tile :],
            tp[:, 2 * tile :],
            t0[:, tile : 2 * tile],
            t0[:, :tile],
            t1[:, tile : 2 * tile],
        ]
    )
    corner = lax.all_gather(lax.psum(corner, COL), "row")
    return (strip, wide, corner)


def shards(kkt, swaps, inverses, pivots, couplings, pattern):
    tile = inverses.shape[1]
    row_groups = lax.axis_size("row")
    x_size = lax.axis_size("col_0")
    z_size = lax.axis_size("col_1")
    row_index = lax.axis_index("row")
    col_index = lax.axis_index(COL)
    rows, source, sliced, partner = plan(swaps, tile, row_groups)
    flat = sliced.reshape(-1)
    owned = flat // tile % row_groups == row_index
    taken = jnp.take(kkt, flat // tile // row_groups * tile + flat % tile, axis=0)
    picked = jnp.where(owned[:, None], taken, 0.0).reshape(row_groups, -1, tile)
    moves = hits(source, col_index * tile, tile).T
    strip, wide, corner = exchange(picked, moves, tile, row_groups, x_size)

    def ordered(piece):
        return piece.reshape(row_groups, 3, -1, tile).transpose(1, 0, 2, 3).reshape(-1, tile)

    corner = corner.transpose(1, 0, 2, 3).reshape(6, tile, tile)
    to_partner = corner[0:3].reshape(3 * tile, tile)
    block_01, block_00, block_11 = (corner[3], corner[4], corner[5])
    tiles = [row_index + row_groups * slot for slot in range(x_size)] + [col_index]
    strips = [ordered(wide[slot]) for slot in range(x_size)] + [ordered(strip)]
    marks = [hits(partner, index * tile, tile) for index in tiles]
    keep = [1.0 - jnp.sum(mark, axis=0) for mark in marks]
    fixed = [
        strips[n] * keep[n][None, :]
        + jnp.dot(to_partner, marks[n], precision=HI, preferred_element_type=jnp.float32)
        for n in range(x_size + 1)
    ]
    upper = [jnp.where(tiles[n] == 1, block_01, fixed[n][:tile]) for n in range(x_size + 1)]
    low0 = [jnp.where(tiles[n] > 0, tdot(inverses[0], upper[n]), 0.0) for n in range(x_size + 1)]
    low0_1 = tdot(inverses[0], block_01)
    scaled0_1 = along_d(low0_1, pivots[0], couplings[0], pattern[0])
    scaled0 = along_d(low0[-1], pivots[0], couplings[0], pattern[0])
    low1 = [
        jnp.where(
            tiles[n] > 1,
            tdot(inverses[1], fixed[n][tile : 2 * tile] - tdot(scaled0_1, low0[n])),
            0.0,
        )
        for n in range(x_size + 1)
    ]
    scaled1 = along_d(low1[-1], pivots[1], couplings[1], pattern[1])
    outs = []
    for n in range(x_size):
        base = kkt[n * tile : (n + 1) * tile] * keep[n][:, None] * keep[-1][None, :]
        base = base + tdot(marks[n], fixed[-1][2 * tile :])
        base = base + tdot(fixed[n][2 * tile :] * keep[n][None, :], marks[-1])
        value = base - tdot(low0[n], scaled0) - tdot(low1[n], scaled1)
        value = jnp.where(tiles[n] == 0, scaled0, value)
        value = jnp.where(tiles[n] == 1, scaled1, value)
        at_0 = jnp.where(tiles[n] == 0, block_00, low0[n].T)
        at_1 = jnp.where(tiles[n] == 0, scaled0_1, low1[n].T)
        at_1 = jnp.where(tiles[n] == 1, block_11 - tdot(low0_1, scaled0_1), at_1)
        value = jnp.where(col_index == 0, at_0, value)
        value = jnp.where(col_index == 1, at_1, value)
        outs.append(value)
    return jnp.concatenate(outs, axis=0)


def solution(mesh):
    z_size = mesh.shape["row"]
    finer = Mesh(mesh.devices.reshape(mesh.shape["row"], -1, z_size), ("row", "col_0", "col_1"))
    in_specs = (P("row", COL), P(), P(), P(), P(), P())
    return jax.shard_map(
        shards, mesh=finer, in_specs=in_specs, out_specs=P("row", COL), check_vma=False
    )
```

profile of v0, /device:TPU:1, one launch (start us, length us, event | category | flops | bytes accessed | tf_op | source)
XLA Modules:
  0.0 369.6 jit_solution(7685777161819229525)
XLA Ops:
  6.5 0.8 slice_bitcast_fusion.9
  7.3 0.7 slice.199
  9.6 3.3 gather_fusion
  12.9 1.2 select_select_fusion
  14.2 35.9 %reduce-scatter.2.cloned.1.call-done = f32[1,96,256]{2,1,0:T(8,128)} async-done(((f32[8,96,256]{2,1,0:T(8,128)}), f32[1,96,256]{2,1,0:T(8,128)}) %reduce-scatter.2.cloned.1.call-update) | async-done | bytes 98320 | tf_op jit(solution)/shard_map/reduce_scatter | solution.py:56
  50.1 1.5 fusion.17
  51.6 0.7 copy-done.4
  52.4 16.4 %all_gather.17 = f32[8,96,256]{2,1,0:T(8,128)S(1)} all-gather(f32[1,96,256]{2,1,0:T(8,128)} %reduce-scatter.2.cloned.1.call-done), channel_id=1, replica_groups=mesh['row'=8,'col_0'=4,'col_1'=8] {'row'}, dimensions={0}, use_global_device_ids=true | all-gather | bytes 884736 | tf_op jit(solution)/shard_map/all_gather | solution.py:57
  68.8 1.0 select_bitcast_fusion
  69.8 124.7 %all-reduce.10.cloned.1.call-done = f32[1,6,32,256]{3,2,1,0:T(8,128)} async-done(((f32[1,6,32,256]{3,2,1,0:T(8,128)}), f32[1,6,32,256]{3,2,1,0:T(8,128)}) %all-reduce.10.cloned.1.call-update) | async-done | bytes 196624 | tf_op jit(solution)/shard_map/psum | solution.py:72
  195.3 73.7 %all-reduce.12.cloned.1.call-done = f32[1,8,96,256]{3,2,1,0:T(8,128)} async-done(((f32[1,8,96,256]{3,2,1,0:T(8,128)}), f32[1,8,96,256]{3,2,1,0:T(8,128)}) %all-reduce.12.cloned.1.call-update) | async-done | bytes 786448 | tf_op jit(solution)/shard_map/psum | solution.py:58
  269.2 31.6 %all-gather.3.cloned.1.call-done = f32[8,6,32,256]{3,2,1,0:T(8,128)} async-done(((f32[1,6,32,256]{3,2,1,0:T(8,128)}), f32[8,6,32,256]{3,2,1,0:T(8,128)}) %all-gather.3.cloned.1.call-update) | async-done | bytes 1572880 | tf_op jit(solution)/shard_map/all_gather | solution.py:72
  300.8 1.5 copy.51
  302.4 0.8 fusion.125
  304.6 0.6 convolution_select_fusion.7
  305.5 0.6 convolution_subtract_fusion.11
  306.1 0.6 fusion.8
  307.3 1.2 convolution_add_fusion.6
  310.0 0.6 convolution_subtract_fusion.13
  310.6 33.6 %all-gather.5.cloned.1.call-done = f32[4,8,96,256]{3,2,1,0:T(8,128)} async-done(((f32[1,8,96,256]{3,2,1,0:T(8,128)}), f32[4,8,96,256]{3,2,1,0:T(8,128)}) %all-gather.5.cloned.1.call-update) | async-done | bytes 3145744 | tf_op jit(solution)/shard_map/all_gather | solution.py:59
  344.2 2.2 fusion.124
  350.0 0.6 convolution_select_fusion.1
  350.6 0.6 convolution_subtract_fusion.2
  351.7 0.6 convolution_select_fusion.3
  352.3 0.8 convolution_subtract_fusion.5
  354.3 0.6 convolution_select_fusion.5
  356.4 0.6 bitcast_select_fusion.3
  358.0 0.6 convolution_select_fusion
  358.6 0.6 convolution_select_fusion.2
  359.2 0.6 convolution_select_fusion.4
  359.8 0.6 convolution_select_fusion.8
  362.1 1.0 pad_maximum_fusion
  (99 shorter events, 15.6 us)
Async XLA Ops:
  6.5 43.5 %reduce-scatter.2.cloned.1.call-start = ((), (), s32[]{:S(2)}) async-start(), calls=%async_computation.1 | async-start | bytes 884736 | tf_op jit(solution)/shard_map/reduce_scatter | solution.py:56
  14.1 180.4 %all-reduce.10.cloned.1.call-start = ((), (), s32[]{:S(2)}) async-start(), calls=%async_computation.2 | async-start | bytes 393216 | tf_op jit(solution)/shard_map/psum | solution.py:72
  51.6 0.7 copy-start.4
  52.3 142.9 %copy-start.5 = (s32[2,256]{1,0:T(2,128)S(1)}, s32[2,256]{1,0:T(2,128)}, u32[]{:S(2)}) copy-start(s32[2,256]{1,0:T(2,128)} %param.11) | copy-start | bytes 6148
  52.3 142.9 %copy-start.6 = (f32[2,256]{1,0:T(2,128)S(1)}, f32[2,256]{1,0:T(2,128)}, u32[]{:S(2)}) copy-start(f32[2,256]{1,0:T(2,128)} %param.10) | copy-start | bytes 6148
  52.4 216.6 %all-reduce.12.cloned.1.call-start = ((), (), s32[]{:S(2)}) async-start(), calls=%async_computation.4 | async-start | bytes 1572864 | tf_op jit(solution)/shard_map/psum | solution.py:58
  68.8 200.2 %copy-start.7 = (f32[2,256]{1,0:T(2,128)S(1)}, f32[2,256]{1,0:T(2,128)}, u32[]{:S(2)}) copy-start(f32[2,256]{1,0:T(2,128)} %param.9) | copy-start | bytes 6148
  69.8 231.1 %all-gather.3.cloned.1.call-start = ((), (), s32[]{:S(2)}) async-start(), calls=%async_computation.3 | async-start | bytes 1769472 | tf_op jit(solution)/shard_map/all_gather | solution.py:72
  194.5 149.6 %all-gather.5.cloned.1.call-start = ((), (), s32[]{:S(2)}) async-start(), calls=%async_computation.5 | async-start | bytes 3932160 | tf_op jit(solution)/shard_map/all_gather | solution.py:59
  302.4 1.0 copy-start.1
  306.1 1.2 copy-start
  348.6 1.0 copy-start.2
  354.9 1.5 copy-start.3
Sparse Core Ops, SparseCore 0:
  14.2 35.8 reduce-scatter.1
  53.5 140.9 all-reduce.9
  196.8 72.0 all-reduce.11
  270.6 30.1 all-gather.2
  302.5 41.6 all-gather.4
where the time goes:
time: 370 us
  waiting for transfers between devices  300 us (81%)
  matrix products  22.2 us (6%)
  blocking collectives  16.4 us (4%)
  between operations  13.9 us (4%)
  local copies, waits for them, and re-layouts  11.6 us (3%)
  other arithmetic  5.64 us (2%)
    psum x1, waiting for transfers between devices, exchange(): corner = lax.all_gather(lax.psum(corner, COL), 'row')  125 us
    psum x1, waiting for transfers between devices, exchange(): mine = lax.psum(jnp.where(z_index == row_index, strip, 0.0), 'col_1')  73.7 us
    reduce_scatter x1, waiting for transfers between devices, exchange(): piece = lax.psum_scatter(picked, 'row', scatter_dimension=0, tiled=False)  35.9 us
    all_gather x1, waiting for transfers between devices, exchange(): wide = lax.all_gather(mine, 'col_0')  33.6 us
    all_gather x1, waiting for transfers between devices, exchange(): corner = lax.all_gather(lax.psum(corner, COL), 'row')  31.6 us
    dot_general x33, matrix products, tdot(): lax.dot_general(a, b, (((0,), (0,)), ((), ())), precision=HI, preferred_e...  17.9 us
    all_gather x1, blocking collectives, exchange(): strip = lax.all_gather(piece, 'row')  16.4 us
  transfers between devices with their start and end apart: 5, of which 5 were waited for; matrix products, arithmetic and copies ran while one was open for 3% of the time, Pallas kernels for 0%

commit v1 on v0

--- a/solution.py
+++ b/solution.py
@@ -69,7 +69,13 @@
             t1[:, tile : 2 * tile],
         ]
     )
-    corner = lax.all_gather(lax.psum(corner, COL), "row")
+
+    def assign_node(local_block):
+        for c in ("col_0", "col_1"):
+            local_block = lax.psum(local_block, c)
+        return local_block
+
+    corner = lax.all_gather(assign_node(corner), "row")
     return (strip, wide, corner)
 
 

time: 370 us -> 276 us (0.75)
  waiting for transfers between devices: 300 us -> 205 us
    psum x2, waiting for transfers between devices: 198 us -> 105 us  [assign_node(): local_block = lax.psum(local_block, c)]
  transfers between devices with their start and end apart: 5 -> 5, of which waited for: 5 -> 5; matrix products, arithmetic and copies ran while one was open for 3% -> 4% of each run, Pallas kernels for 0% -> 0%
where the time goes in v1:
time: 276 us; the launch traced here: 275 us
  waiting for transfers between devices  205 us (74%)
  matrix products  22.2 us (8%)
  blocking collectives  16.4 us (6%)
  between operations  13.9 us (5%)
  local copies, waits for them, and re-layouts  11.6 us (4%)
  other arithmetic  5.64 us (2%)
    psum x2, waiting for transfers between devices, assign_node(): local_block = lax.psum(local_block, c)  105 us
    reduce_scatter x1, waiting for transfers between devices, exchange(): piece = lax.psum_scatter(picked, 'row', scatter_dimension=0, tiled=False)  35.9 us
    all_gather x1, waiting for transfers between devices, exchange(): wide = lax.all_gather(mine, 'col_0')  33.6 us
    all_gather x1, waiting for transfers between devices, exchange(): corner = lax.all_gather(assign_node(corner), 'row')  30.8 us
    dot_general x33, matrix products, tdot(): lax.dot_general(a, b, (((0,), (0,)), ((), ())), precision=HI, preferred_e...  17.9 us
    all_gather x1, blocking collectives, exchange(): strip = lax.all_gather(piece, 'row')  16.4 us
  transfers between devices with their start and end apart: 5, of which 5 were waited for; matrix products, arithmetic and copies ran while one was open for 4% of the time, Pallas kernels for 0%

profile of v1, /device:TPU:1, one launch (start us, length us, event | category | flops | bytes accessed | tf_op | source)
XLA Modules:
  0.0 275.2 jit_solution(16788505355199296939)
XLA Ops:
  6.5 0.8 slice_bitcast_fusion.9
  7.3 0.7 slice.199
  9.6 3.3 %gather_fusion = f32[768,256]{1,0:T(8,128)S(1)} fusion(f32[1024,256]{1,0:T(8,128)} %param.6, s32[1024]{0:T(1024)S(1)} %pad_clamp_fusion), kind=kCustom, calls=%fused_computation | custom fusion | bytes 1575936 | tf_op jit(solution)/shard_map/jit(_take)/gather | solution.py:92
  12.9 1.2 select_select_fusion
  14.2 35.9 %reduce-scatter.2.cloned.1.call-done = f32[1,96,256]{2,1,0:T(8,128)} async-done(((f32[8,96,256]{2,1,0:T(8,128)}), f32[1,96,256]{2,1,0:T(8,128)}) %reduce-scatter.2.cloned.1.call-update) | async-done | bytes 98320 | tf_op jit(solution)/shard_map/reduce_scatter | solution.py:56
  50.1 1.5 fusion.17
  51.6 0.7 copy-done.4
  52.4 16.4 %all_gather.17 = f32[8,96,256]{2,1,0:T(8,128)S(1)} all-gather(f32[1,96,256]{2,1,0:T(8,128)} %reduce-scatter.2.cloned.1.call-done), channel_id=1, replica_groups=mesh['row'=8,'col_0'=4,'col_1'=8] {'row'}, dimensions={0}, use_global_device_ids=true | all-gather | bytes 884736 | tf_op jit(solution)/shard_map/all_gather | solution.py:57
  68.8 1.0 select_bitcast_fusion
  69.7 28.5 %all-reduce.11.cloned.1.call-done = f32[6,32,256]{2,1,0:T(8,128)} async-done(((f32[6,32,256]{2,1,0:T(8,128)}), f32[6,32,256]{2,1,0:T(8,128)}) %all-reduce.11.cloned.1.call-update) | async-done | bytes 196624 | tf_op jit(solution)/shard_map/psum | solution.py:75
  98.3 76.3 %all-reduce.13.cloned.1.call-done = (f32[1,6,32,256]{3,2,1,0:T(8,128)}, f32[1,8,96,256]{3,2,1,0:T(8,128)}) async-done(((f32[1,6,32,256]{3,2,1,0:T(8,128)}, f32[1,8,96,256]{3,2,1,0:T(8,128)}), (f32[1,6,32,256]{3,2,1,0:T(8,128)}, f32[1,8,96,256]{3,2,1,0:T(8,128)})) %all-reduce.13.cloned.1.call-update) | async-done | bytes 983056 | tf_op jit(solution)/shard_map/psum | solution.py:75
  175.6 30.8 %all-gather.3.cloned.1.call-done = f32[8,6,32,256]{3,2,1,0:T(8,128)} async-done(((f32[1,6,32,256]{3,2,1,0:T(8,128)}), f32[8,6,32,256]{3,2,1,0:T(8,128)}) %all-gather.3.cloned.1.call-update) | async-done | bytes 1572880 | tf_op jit(solution)/shard_map/all_gather | solution.py:78
  206.4 1.5 copy.51
  208.0 0.8 fusion.125
  210.1 0.6 convolution_select_fusion.7
  211.0 0.6 convolution_subtract_fusion.11
  211.6 0.6 fusion.8
  212.9 1.2 convolution_add_fusion.6
  215.5 0.6 convolution_subtract_fusion.13
  216.1 33.6 %all-gather.5.cloned.1.call-done = f32[4,8,96,256]{3,2,1,0:T(8,128)} async-done(((f32[1,8,96,256]{3,2,1,0:T(8,128)}), f32[4,8,96,256]{3,2,1,0:T(8,128)}) %all-gather.5.cloned.1.call-update) | async-done | bytes 3145744 | tf_op jit(solution)/shard_map/all_gather | solution.py:59
  249.7 2.2 fusion.124
  255.6 0.6 convolution_select_fusion.1
  256.2 0.6 convolution_subtract_fusion.2
  257.2 0.6 convolution_select_fusion.3
  257.8 0.8 convolution_subtract_fusion.5
  259.9 0.6 convolution_select_fusion.5
  262.0 0.6 bitcast_select_fusion.3
  263.6 0.6 convolution_select_fusion
  264.2 0.6 convolution_select_fusion.2
  264.8 0.6 convolution_select_fusion.4
  265.4 0.6 convolution_select_fusion.8
  267.6 1.0 pad_maximum_fusion
  (99 shorter events, 15.6 us)
Async XLA Ops:
  6.5 43.5 %reduce-scatter.2.cloned.1.call-start = ((), (), s32[]{:S(2)}) async-start(), calls=%async_computation.1 | async-start | bytes 884736 | tf_op jit(solution)/shard_map/reduce_scatter | solution.py:56
  14.1 84.1 %all-reduce.11.cloned.1.call-start = ((), (), s32[]{:S(2)}) async-start(), calls=%async_computation.2 | async-start | bytes 393216 | tf_op jit(solution)/shard_map/psum | solution.py:75
  51.6 0.7 copy-start.4
  52.3 122.2 %all-reduce.13.cloned.1.call-start = ((), (), s32[]{:S(2)}) async-start(), calls=%async_computation.5 | async-start | bytes 1966080 | tf_op jit(solution)/shard_map/psum | solution.py:75
  68.8 106.5 %copy-start.5 = (s32[2,256]{1,0:T(2,128)S(1)}, s32[2,256]{1,0:T(2,128)}, u32[]{:S(2)}) copy-start(s32[2,256]{1,0:T(2,128)} %param.11) | copy-start | bytes 6148
  68.8 106.5 %copy-start.6 = (f32[2,256]{1,0:T(2,128)S(1)}, f32[2,256]{1,0:T(2,128)}, u32[]{:S(2)}) copy-start(f32[2,256]{1,0:T(2,128)} %param.10) | copy-start | bytes 6148
  68.8 106.7 %copy-start.7 = (f32[2,256]{1,0:T(2,128)S(1)}, f32[2,256]{1,0:T(2,128)}, u32[]{:S(2)}) copy-start(f32[2,256]{1,0:T(2,128)} %param.9) | copy-start | bytes 6148
  98.2 108.1 %all-gather.3.cloned.1.call-start = ((), (), s32[]{:S(2)}) async-start(), calls=%async_computation.3 | async-start | bytes 1769472 | tf_op jit(solution)/shard_map/all_gather | solution.py:78
  174.6 75.1 %all-gather.5.cloned.1.call-start = ((), (), s32[]{:S(2)}) async-start(), calls=%async_computation.4 | async-start | bytes 3932160 | tf_op jit(solution)/shard_map/all_gather | solution.py:59
  207.9 1.0 copy-start.1
  211.6 1.2 copy-start
  254.2 1.0 copy-start.2
  260.5 1.5 copy-start.3
Sparse Core Ops, SparseCore 0:
  14.2 35.8 reduce-scatter.1
  52.5 45.7 all-reduce.10
  100.7 73.8 all-reduce.12
  176.3 30.0 all-gather.2
  208.0 41.6 all-gather.4

commit v2 on v0

--- a/solution.py
+++ b/solution.py
@@ -55,7 +55,9 @@
     z_index = lax.axis_index("col_1")
     piece = lax.psum_scatter(picked, "row", scatter_dimension=0, tiled=False)
     strip = lax.all_gather(piece, "row")
-    mine = lax.psum(jnp.where(z_index == row_index, strip, 0.0), "col_1")
+    block = jnp.where(z_index == row_index, strip, 0.0)
+    parts = lax.all_gather(block, "col_1")
+    mine = jnp.sum(parts, axis=0)
     wide = lax.all_gather(mine, "col_0")
     part = jnp.dot(piece, moves, precision=HI, preferred_element_type=jnp.float32)
     t0, t1, tp = (part[:width], part[width : 2 * width], part[2 * width :])

time: 370 us -> 369 us (level)
  waiting for transfers between devices: 300 us -> 295 us
  other arithmetic: 5.64 us -> 9.82 us
    all_gather x0 -> x1, waiting for transfers between devices: none -> 77.2 us  [exchange(): parts = lax.all_gather(block, 'col_1')]
    psum x1 -> x0, waiting for transfers between devices: 73.7 us -> none  [exchange(): mine = lax.psum(jnp.where(z_index == row_index, strip, 0.0), 'col_1')]
    all_gather x1, waiting for transfers between devices: 31.6 us -> 23.3 us  [exchange(): corner = lax.all_gather(lax.psum(corner, COL), 'row')]
    reduce_sum x0 -> x1, other arithmetic: none -> 4.18 us  [exchange(): mine = jnp.sum(parts, axis=0)]
  transfers between devices with their start and end apart: 5 -> 5, of which waited for: 5 -> 5; matrix products, arithmetic and copies ran while one was open for 3% -> 4% of each run, Pallas kernels for 0% -> 0%
where the time goes in v2:
time: 369 us
  waiting for transfers between devices  295 us (80%)
  matrix products  22.2 us (6%)
  blocking collectives  16.4 us (4%)
  between operations  13.9 us (4%)
  local copies, waits for them, and re-layouts  10.7 us (3%)
  other arithmetic  9.82 us (3%)
    psum x1, waiting for transfers between devices, exchange(): corner = lax.all_gather(lax.psum(corner, COL), 'row')  125 us
    all_gather x1, waiting for transfers between devices, exchange(): parts = lax.all_gather(block, 'col_1')  77.2 us
    reduce_scatter x1, waiting for transfers between devices, exchange(): piece = lax.psum_scatter(picked, 'row', scatter_dimension=0, tiled=False)  35.9 us
    all_gather x1, waiting for transfers between devices, exchange(): wide = lax.all_gather(mine, 'col_0')  34.2 us
    all_gather x1, waiting for transfers between devices, exchange(): corner = lax.all_gather(lax.psum(corner, COL), 'row')  23.3 us
    dot_general x33, matrix products, tdot(): lax.dot_general(a, b, (((0,), (0,)), ((), ())), precision=HI, preferred_e...  17.9 us
    all_gather x1, blocking collectives, exchange(): strip = lax.all_gather(piece, 'row')  16.4 us
  transfers between devices with their start and end apart: 5, of which 5 were waited for; matrix products, arithmetic and copies ran while one was open for 4% of the time, Pallas kernels for 0%

profile of v2, /device:TPU:1, one launch (start us, length us, event | category | flops | bytes accessed | tf_op | source)
XLA Modules:
  0.0 368.7 jit_solution(3839044218326096964)
XLA Ops:
  6.5 0.7 slice.199
  7.2 0.8 slice_bitcast_fusion.9
  9.6 3.3 gather_fusion
  12.9 1.2 select_select_fusion
  14.2 35.9 %reduce-scatter.2.cloned.1.call-done = f32[1,96,256]{2,1,0:T(8,128)} async-done(((f32[8,96,256]{2,1,0:T(8,128)}), f32[1,96,256]{2,1,0:T(8,128)}) %reduce-scatter.2.cloned.1.call-update) | async-done | bytes 98320 | tf_op jit(solution)/shard_map/reduce_scatter | solution.py:56
  50.1 1.5 fusion.17
  51.7 0.7 copy-done.4
  52.4 16.4 %all_gather.23 = f32[8,96,256]{2,1,0:T(8,128)S(1)} all-gather(f32[1,96,256]{2,1,0:T(8,128)} %reduce-scatter.2.cloned.1.call-done), channel_id=1, replica_groups=mesh['row'=8,'col_0'=4,'col_1'=8] {'row'}, dimensions={0}, use_global_device_ids=true | all-gather | bytes 884736 | tf_op jit(solution)/shard_map/all_gather | solution.py:57
  68.8 1.0 broadcast_select_fusion
  69.8 124.7 %all-reduce.9.cloned.1.call-done = f32[1,6,32,256]{3,2,1,0:T(8,128)} async-done(((f32[1,6,32,256]{3,2,1,0:T(8,128)}), f32[1,6,32,256]{3,2,1,0:T(8,128)}) %all-reduce.9.cloned.1.call-update) | async-done | bytes 196624 | tf_op jit(solution)/shard_map/psum | solution.py:74
  195.3 77.2 %all-gather.8.cloned.1.call-done = f32[64,96,256]{2,1,0:T(8,128)} async-done(((f32[8,96,256]{2,1,0:T(8,128)}), f32[64,96,256]{2,1,0:T(8,128)}) %all-gather.8.cloned.1.call-update) | async-done | bytes 6291472 | tf_op jit(solution)/shard_map/all_gather | solution.py:59
  272.5 4.2 %reduce_sum.74 = f32[8,96,256]{2,1,0:T(8,128)} reduce(f32[8,8,96,256]{3,2,1,0:T(8,128)} %bitcast.169, f32[]{:T(128)} %constant.92.clone.1), dimensions={0}, to_apply=%region_6.7 | reduce | flops 1376256 | bytes 7077892 | tf_op jit(solution)/shard_map/reduce_sum | solution.py:60
  277.0 23.3 %all-gather.6.cloned.1.call-done = f32[8,6,32,256]{3,2,1,0:T(8,128)} async-done(((f32[1,6,32,256]{3,2,1,0:T(8,128)}), f32[8,6,32,256]{3,2,1,0:T(8,128)}) %all-gather.6.cloned.1.call-update) | async-done | bytes 1572880 | tf_op jit(solution)/shard_map/all_gather | solution.py:74
  300.3 1.5 copy.52
  301.9 0.8 fusion.125
  302.7 0.6 fusion.55
  303.8 0.6 convolution_select_fusion.7
  304.7 0.6 convolution_subtract_fusion.11
  305.3 0.6 fusion.8
  307.6 1.2 convolution_add_fusion.6
  308.8 0.6 convolution_subtract_fusion.13
  309.4 34.2 %all-gather.10.cloned.1.call-done = f32[32,96,256]{2,1,0:T(8,128)} async-done(((f32[8,96,256]{2,1,0:T(8,128)}), f32[32,96,256]{2,1,0:T(8,128)}) %all-gather.10.cloned.1.call-update) | async-done | bytes 3145744 | tf_op jit(solution)/shard_map/all_gather | solution.py:61
  343.6 2.2 fusion.124
  349.1 0.6 convolution_select_fusion.1
  350.7 0.8 convolution_select_fusion.3
  352.6 0.6 convolution_select_fusion.5
  354.3 0.6 bitcast_select_fusion.3
  357.1 0.6 convolution_select_fusion.8
  357.7 0.6 convolution_select_fusion.4
  358.3 0.6 convolution_select_fusion.2
  358.9 0.6 convolution_select_fusion
  361.1 1.0 pad_maximum_fusion
  (100 shorter events, 15.2 us)
Async XLA Ops:
  6.5 43.6 %reduce-scatter.2.cloned.1.call-start = ((), (), s32[]{:S(2)}) async-start(), calls=%async_computation.1 | async-start | bytes 884736 | tf_op jit(solution)/shard_map/reduce_scatter | solution.py:56
  12.9 182.3 %copy-start.5 = (s32[2,256]{1,0:T(2,128)S(1)}, s32[2,256]{1,0:T(2,128)}, u32[]{:S(2)}) copy-start(s32[2,256]{1,0:T(2,128)} %param.11) | copy-start | bytes 6148
  12.9 182.3 %copy-start.6 = (f32[2,256]{1,0:T(2,128)S(1)}, f32[2,256]{1,0:T(2,128)}, u32[]{:S(2)}) copy-start(f32[2,256]{1,0:T(2,128)} %param.10) | copy-start | bytes 6148
  14.1 180.4 %all-reduce.9.cloned.1.call-start = ((), (), s32[]{:S(2)}) async-start(), calls=%async_computation.2 | async-start | bytes 393216 | tf_op jit(solution)/shard_map/psum | solution.py:74
  51.7 0.7 copy-start.4
  52.4 220.2 %all-gather.8.cloned.1.call-start = ((), (), s32[]{:S(2)}) async-start(), calls=%async_computation.4 | async-start | bytes 7077888 | tf_op jit(solution)/shard_map/all_gather | solution.py:59
  69.8 230.5 %all-gather.6.cloned.1.call-start = ((), (), s32[]{:S(2)}) async-start(), calls=%async_computation.3 | async-start | bytes 1769472 | tf_op jit(solution)/shard_map/all_gather | solution.py:74
  194.5 149.1 %all-gather.10.cloned.1.call-start = ((), (), s32[]{:S(2)}) async-start(), calls=%async_computation.5 | async-start | bytes 3932160 | tf_op jit(solution)/shard_map/all_gather | solution.py:61
  272.5 4.3 %copy-start.7 = (f32[2,256]{1,0:T(2,128)S(1)}, f32[2,256]{1,0:T(2,128)}, u32[]{:S(2)}) copy-start(f32[2,256]{1,0:T(2,128)} %param.9) | copy-start | bytes 6148
  277.0 25.7 %copy-start.1 = (f32[2,256,256]{2,1,0:T(8,128)S(1)}, f32[2,256,256]{2,1,0:T(8,128)}, u32[]{:S(2)}) copy-start(f32[2,256,256]{2,1,0:T(8,128)} %param.8) | copy-start | bytes 1572868
  304.5 1.6 copy-start
  346.9 1.7 copy-start.2
  350.3 4.0 %copy-start.3 = (f32[1,8,32,256]{3,2,1,0:T(8,128)S(1)}, f32[1,8,32,256]{3,2,1,0:T(8,128)}, u32[]{:S(2)}) copy-start(f32[1,8,32,256]{3,2,1,0:T(8,128)} %get-tuple-element.15) | copy-start | bytes 786436
Sparse Core Ops, SparseCore 0:
  14.2 35.8 reduce-scatter.1
  53.5 140.9 all-reduce.8
  196.3 76.1 all-gather.7
  274.2 26.0 all-gather.5
  301.9 41.6 all-gather.9
